TPU v7x, 256 devices: a whole 4x4x8 slice. The times are simulated.
256 devices in a mesh: leaf: 64 (over z, y, core), samp: 4 (over x).
Axes of the slice: x: 4, y: 4, z: 8, core: 2. Of those that a mesh axis runs over, the one named last changes fastest.
Arguments:
- points: bfloat16 [8, 131072], P(None, 'leaf'), may hold values from -6 to 6
- omega: bfloat16 [131072, 512], P('leaf', 'samp'), may hold values from -1.1953125 to 1.1953125
- near_lists: int32 [256, 8], replicated, may hold values from 0 to 255, as said below
- leaf_order: int32 [256], replicated, may hold values from 0 to 255, as said below
- pivots: int32 [256, 128], P('leaf'), may hold values from 0 to 511, as said below
Outputs:
- interpolation: bfloat16 [131072, 128], P('leaf')
- parent_rows: float32 [32768, 512], P('leaf', 'samp')
Inputs may be any that keep to these rules, and one draw needn't show every extreme that they name: `near_lists`: entries of a row are distinct initial leaf numbers. Mapped through leaf_order, the rows of one aligned block of 4 tree-order leaves name at most 2 distinct leaves of any one aligned block of 4 tree-order leaves, and exactly 2 for some such block; a leaf may be named in several rows. `leaf_order`: A permutation. `pivots`: entries of a row are distinct.
All inputs are finite; a program needn't handle non-finite values.
Results may differ from a plain program's by a relative error of at most 0.013.
Values may be sent and summed in bfloat16 or wider, within the bound.
No kernel may reach another device: no remote copies, remote signals or barrier semaphores. Data moves between devices by JAX's collectives and lax.ppermute only.
A program may use at most 128 MiB of HBM per device.

v0:
```python
import functools

import jax
import jax.numpy as jnp
from jax import lax
from jax.experimental import pallas as pl
from jax.experimental.pallas import tpu as pltpu
from jax.sharding import PartitionSpec as P


DIMS = 8
LEAF_PTS = 512
NEAR = 8
SKEL = 128
SLOTS = 2
LEAF_DEV = 4
REACH = 3
LEAVES = 256
NODES = LEAVES // LEAF_DEV
RIDGE = 0.1
RATE = 0.25

AUG = 16
PACK = LEAF_PTS + DIMS * LEAF_PTS // 128
SIBLING, BEHIND, BEHIND_ACROSS, AHEAD, MIXED, FAR = (1, -1), (-2, -2), (-1, -3), (2, 2), (-3, 1), (NODES // 2, NODES // 2)
OFFSETS = (BEHIND, BEHIND_ACROSS, AHEAD, MIXED, SIBLING, FAR)
CLASSES = len(OFFSETS)
HALF = CLASSES - 1
BESIDE = CLASSES - 2
GROUPS = ((4, 0, 1), (2, 3), (HALF,))
FIRST, SECOND = (0,), (1, 2, 3)
T_LEAF = 96
T_OK = 0
T_OWN = 8
T_FAR = 32
T_LEN = 128
VMEM_LIMIT = 16 << 20

VMEM = pltpu.VMEM
SMEM = pltpu.SMEM
F32 = jnp.float32
BF16 = jnp.bfloat16
HIGHEST = lax.Precision.HIGHEST


def vm(count):
    return [pl.BlockSpec(memory_space=VMEM)] * count


def dot_tn(a, b):
    return lax.dot_general(a, b, (((0,), (0,)), ((), ())), preferred_element_type=F32)


def dot_nt(a, b):
    return lax.dot_general(a, b, (((1,), (1,)), ((), ())), preferred_element_type=F32)


def split_norm(coords):
    norm = RATE * jnp.sum(coords * coords, axis=0, keepdims=True)
    high = norm.astype(BF16).astype(F32)
    rest = norm - high
    middle = rest.astype(BF16).astype(F32)
    low = rest - middle
    return high, middle, low


def left_side(coords):
    high, middle, low = split_norm(coords)
    row = lax.broadcasted_iota(jnp.int32, (DIMS, coords.shape[1]), 0)
    extra = jnp.where(row == 0, -high, jnp.where(row == 1, -middle, jnp.where(row == 2, -low, jnp.where(row < 6, 1.0, 0.0))))
    return jnp.concatenate([coords * (2.0 * RATE), extra], axis=0).astype(BF16)


def right_side(coords):
    high, middle, low = split_norm(coords)
    row = lax.broadcasted_iota(jnp.int32, (DIMS, coords.shape[1]), 0)
    extra = jnp.where(row == 3, -high, jnp.where(row == 4, -middle, jnp.where(row == 5, -low, jnp.where(row < 3, 1.0, 0.0))))
    return jnp.concatenate([coords, extra], axis=0).astype(BF16)


def fill_pack(pack, leaves, points, omega):
    for slot, leaf in enumerate(leaves):
        pack[slot, 0:LEAF_PTS, :] = omega[leaf]
        mine = points[:, pl.ds(pl.multiple_of(leaf * LEAF_PTS, LEAF_PTS), LEAF_PTS)]
        for piece in range(LEAF_PTS // 128):
            pack[slot, LEAF_PTS + DIMS * piece:LEAF_PTS + DIMS * (piece + 1), :] = mine[:, 128 * piece:128 * (piece + 1)]


def send_kernel(near_s, order_s, near_v, order_v, points, omega, table, *packs):
    me = lax.axis_index("leaf")
    halves = [jnp.broadcast_to(order_v[part:part + 1, :], (NEAR, 128)) for part in range(LEAVES // 128)]

    def look(near):
        found = jnp.zeros((NEAR, 128), jnp.int32)
        for part, half in enumerate(halves):
            here = jnp.take_along_axis(half, near & 127, axis=1, mode="promise_in_bounds")
            found = jnp.where(near >> 7 == part, here, found)
        return found

    near = near_v[...]
    tree = jnp.concatenate([look(near[:, 128 * part:128 * (part + 1)]) for part in range(LEAVES // 128)], axis=1)
    node = lax.broadcasted_iota(jnp.int32, (NEAR, LEAVES), 1) >> 2
    part = tree & 3
    weight = jnp.where(part == 0, 1.0, jnp.where(part == 1, 8.0, jnp.where(part == 2, 64.0, 512.0)))
    weight = jnp.where((tree >> 2) == me, weight, 0.0)
    for index, offset in enumerate(OFFSETS):
        even, odd = offset
        requester = (me - jnp.where((me ^ even) & 1 > 0, odd, even)) & (NODES - 1)
        counts = jnp.sum(jnp.where(node == requester, weight, 0.0)).astype(jnp.int32)
        has = [(counts >> (3 * leaf)) & 7 > 0 for leaf in range(LEAF_DEV)]
        first = jnp.where(has[0], 0, jnp.where(has[1], 1, jnp.where(has[2], 2, jnp.where(has[3], 3, 0))))
        second = jnp.where(has[3], 3, jnp.where(has[2], 2, jnp.where(has[1], 1, 0)))
        if index >= BESIDE:
            table[T_LEAF + 2 * index], table[T_LEAF + 2 * index + 1] = first, second
        else:
            fill_pack(packs[index], (first, second), points, omega)

    place = ((tree >> 2) - node + REACH) & (NODES - 1)
    bad = jnp.logical_and(place >= 2 * REACH, place != REACH + NODES // 2)
    table[T_OK] = jnp.where(jnp.max(jnp.where(bad, 1.0, 0.0)) > 0.0, 0, 1)

    def lowest(mask):
        return jnp.where(mask & 1 > 0, 0, jnp.where(mask & 2 > 0, 1, jnp.where(mask & 4 > 0, 2, jnp.where(mask & 8 > 0, 3, 0))))

    def highest(mask):
        return jnp.where(mask & 8 > 0, 3, jnp.where(mask & 4 > 0, 2, jnp.where(mask & 2 > 0, 1, 0)))

    masks = []
    for member in range(LEAF_DEV):
        mask = jnp.int32(0)
        for entry in range(NEAR):
            leaf = order_s[near_s[entry, me * LEAF_DEV + member]]
            spot = ((leaf >> 2) - me + REACH) & (NODES - 1)
            spot = jnp.where(spot < 2 * REACH, spot, 2 * REACH)
            mask = mask | (jnp.int32(1) << (4 * spot + (leaf & 3)))
        masks.append(mask)
    every = masks[0] | masks[1] | masks[2] | masks[3]
    for member in range(LEAF_DEV):
        for source in range(LEAF_DEV):
            table[T_OWN + LEAF_DEV * member + source] = (masks[member] >> (4 * REACH + source)) & 1
    for index, offset in enumerate(OFFSETS):
        spot = 2 * REACH if index == HALF else jnp.where(me & 1 > 0, offset[1], offset[0]) + REACH
        four = (every >> (4 * spot)) & 15
        first, second = lowest(four), highest(four)
        for member in range(LEAF_DEV):
            bits = masks[member] >> (4 * spot)
            table[T_FAR + 8 * index + 2 * member] = (bits >> first) & 1
            table[T_FAR + 8 * index + 2 * member + 1] = jnp.where(first == second, 0, (bits >> second) & 1)


def add_tile(left, right, samples, total, member):
    start = pl.multiple_of(member * LEAF_PTS, LEAF_PTS)
    exponent = jnp.dot(left[pl.ds(start, LEAF_PTS), :], right, preferred_element_type=F32)
    tile = jnp.exp(exponent).astype(BF16)
    total[member] += jnp.dot(tile, samples, preferred_element_type=F32)


def own_kernel(table, points, omega, total, left):
    for member in range(LEAF_DEV):
        coords = points[:, member * LEAF_PTS:(member + 1) * LEAF_PTS]
        left[member * LEAF_PTS:(member + 1) * LEAF_PTS, :] = left_side(coords.astype(F32)).astype(F32).T.astype(BF16)
    total[...] = jnp.zeros_like(total)

    def source_step(source, carry):
        coords = points[:, pl.ds(pl.multiple_of(source * LEAF_PTS, LEAF_PTS), LEAF_PTS)]
        right = right_side(coords.astype(F32))
        samples = omega[source]

        def member_step(member, inner):
            @pl.when(table[T_OWN + LEAF_DEV * member + source] > 0)
            def _():
                add_tile(left, right, samples, total, member)

            return inner

        return lax.fori_loop(0, LEAF_DEV, member_step, carry)

    lax.fori_loop(0, LEAF_DEV, source_step, 0)


def half_kernel(table, points, omega, pivots, left, behind, skeleton, beside, half):
    del left, behind
    for index, pack in ((BESIDE, beside), (HALF, half)):
        fill_pack(pack, (table[T_LEAF + 2 * index], table[T_LEAF + 2 * index + 1]), points, omega)
    for member in range(LEAF_DEV):
        coords = points[:, member * LEAF_PTS:(member + 1) * LEAF_PTS]
        chosen = lax.broadcasted_iota(jnp.int32, (LEAF_PTS, SKEL), 0) == pivots[member:member + 1, :]
        picked = jnp.dot(coords, jnp.where(chosen, 1.0, 0.0).astype(BF16), preferred_element_type=F32).astype(BF16)
        skeleton[:, member * SKEL:(member + 1) * SKEL] = picked
        slot, row = divmod(member, SLOTS)
        beside[slot, PACK + DIMS * row:PACK + DIMS * (row + 1), :] = picked


def add_packs(group, table, left, packs, total):
    for index, pack in zip(group, packs):

        def slot_step(slot, carry, index=index, pack=pack):
            pieces = [pack[slot, LEAF_PTS + DIMS * c:LEAF_PTS + DIMS * (c + 1), :] for c in range(LEAF_PTS // 128)]
            coords = jnp.concatenate([p.astype(F32) for p in pieces], axis=1)
            right = right_side(coords)
            samples = pack[slot, 0:LEAF_PTS, :]

            def member_step(member, inner):
                @pl.when(table[T_FAR + 8 * index + 2 * member + slot] > 0)
                def _():
                    add_tile(left, right, samples, total, member)

                return inner

            return lax.fori_loop(0, LEAF_DEV, member_step, carry)

        lax.fori_loop(0, SLOTS, slot_step, 0)


def early_kernel(group, table, left, before, *rest):
    packs, (total,) = rest[:len(group)], rest[len(group):]
    total[...] = before[...]
    add_packs(group, table, left, packs, total)


def couple_kernel(group, table, left, before, skeleton, beside, *rest):
    packs, (total, coupling) = rest[:len(group)], rest[len(group):]
    early_kernel(group, table, left, before, *packs, total)
    places = [divmod(member, SLOTS) for member in range(LEAF_DEV)]
    pieces = [beside[slot, PACK + DIMS * row:PACK + DIMS * (row + 1), :] for slot, row in places]
    sibling = jnp.concatenate([piece.astype(F32) for piece in pieces], axis=1)
    exponent = dot_tn(left_side(skeleton[...].astype(F32)), right_side(sibling))
    coupling[...] = jnp.exp(exponent).astype(BF16)


def late_kernel(group, table, left, before, *rest):
    packs, (total, *blocks) = rest[:len(group)], rest[len(group):]
    total[...] = before[...]
    add_packs(group, table, left, packs, total)
    column = lax.axis_index("samp")
    for step in range(4):
        blocks[step][...] = total[(column + step) & 3].astype(BF16)


def rows_kernel(total, pivots, rows):
    for member in range(LEAF_DEV):
        chosen = lax.broadcasted_iota(jnp.int32, (LEAF_PTS, SKEL), 0) == pivots[member:member + 1, :]
        pick = jnp.where(chosen, 1.0, 0.0)
        values = total[member]
        rows[member * SKEL:(member + 1) * SKEL, :] = lax.dot_general(pick, values, (((0,), (0,)), ((), ())), preferred_element_type=F32, precision=HIGHEST)


def matmul3(a, b):
    a_high = a.astype(BF16)
    a_low = (a - a_high.astype(F32)).astype(BF16)
    b_high = b.astype(BF16)
    b_low = (b - b_high.astype(F32)).astype(BF16)
    left = jnp.concatenate([a_high, a_high, a_low], axis=1)
    right = jnp.concatenate([b_high, b_low, b_high], axis=0)
    return jnp.dot(left, right, preferred_element_type=F32)


def inverse(gram):
    row = lax.broadcasted_iota(jnp.int32, (SKEL, SKEL), 0)
    eye = jnp.where(row == lax.broadcasted_iota(jnp.int32, (SKEL, SKEL), 1), 1.0, 0.0)
    trace = jnp.sum(jnp.sum(gram * eye, axis=1, keepdims=True), axis=0, keepdims=True)
    shift = RIDGE * trace / SKEL
    scaled = gram / shift + eye
    spread = 1.0 + SKEL / RIDGE
    error = (spread - 1.0) / (spread + 1.0)
    start = 2.0 / (1.0 + spread)
    guess = start * (2.0 * eye - start * scaled)
    error = error * error
    while error > 1e-5:
        factor = 2.0 / (2.0 - error)
        guess = guess * factor
        error = error / (2.0 - error)
        late = error < 0.1
        multiply = functools.partial(jnp.dot, precision=HIGHEST, preferred_element_type=F32) if late else matmul3
        guess = 2.0 * guess - multiply(guess, multiply(scaled, guess))
        error = error * error
    return guess / shift


def solve_kernel(b0, b1, b2, b3, pivots, rows, interpolation):
    del rows
    column = lax.axis_index("samp")
    mine = pivots[pl.ds(column, 1), :]
    chosen = lax.broadcasted_iota(jnp.int32, (LEAF_PTS, SKEL), 0) == mine
    pick = jnp.where(chosen, 1.0, 0.0).astype(BF16)
    gram = jnp.zeros((SKEL, SKEL), F32)
    cross = jnp.zeros((LEAF_PTS, SKEL), F32)
    for block in (b0, b1, b2, b3):
        values = block[...]
        rows = dot_tn(pick, values).astype(BF16)
        gram += dot_nt(rows, rows)
        cross += dot_nt(values, rows)
    interpolation[...] = jnp.dot(cross, inverse(gram), precision=HIGHEST, preferred_element_type=F32).astype(BF16)


def project_kernel(steps, omega, *rest):
    column = lax.axis_index("samp")
    projected = rest[-1]
    if len(rest) > len(steps) + 1:
        projected[...] = rest[0][...]
    for step, block in zip(steps, rest[-1 - len(steps):-1]):
        leaf = (column - step) & 3
        spot = pl.ds(pl.multiple_of(leaf * SKEL, SKEL), SKEL)
        projected[spot, :] = dot_tn(block[...], omega[leaf]).astype(BF16)


def stack_kernel(i0, i1, i2, i3, interpolation):
    column = lax.axis_index("samp")
    for step, block in enumerate((i0, i1, i2, i3)):
        leaf = (column - step) & 3
        interpolation[pl.ds(pl.multiple_of(leaf * LEAF_PTS, LEAF_PTS), LEAF_PTS), :] = block[...]


def parent_kernel(rows, coupling, projected, parent):
    parent[...] = rows[...] - jnp.dot(coupling[...], projected[...], preferred_element_type=F32)


def kernel_tile(own, far):
    own_f, far_f = own.astype(F32), far.astype(F32)
    inner = jnp.dot(own.T, far, preferred_element_type=F32)
    distance = jnp.sum(own_f * own_f, 0)[:, None] + jnp.sum(far_f * far_f, 0)[None, :] - 2.0 * inner
    return jnp.exp(-RATE * distance).astype(BF16)


def general_sample(points, omega, near_lists, leaf_order):
    nodes = lax.axis_size("leaf")
    me = lax.axis_index("leaf")
    columns = omega.shape[1]
    references = LEAF_DEV * NEAR
    tree = jnp.take(leaf_order, near_lists, axis=0).reshape(nodes, references)
    leaf = lax.broadcasted_iota(jnp.int32, (1, 1, LEAF_DEV), 2)
    wants = jnp.any(tree[:, :, None] == me * LEAF_DEV + leaf, axis=1)
    first = jnp.argmax(wants, axis=1).astype(jnp.int32)
    second = (LEAF_DEV - 1 - jnp.argmax(wants[:, ::-1], axis=1)).astype(jnp.int32)
    send = jnp.stack([first, second], axis=1).reshape(-1)
    leaf_points = jnp.moveaxis(points.reshape(DIMS, LEAF_DEV, LEAF_PTS), 1, 0)
    got_points = lax.all_to_all(jnp.take(leaf_points, send, axis=0), "leaf", 0, 0, tiled=True)
    got_samples = lax.all_to_all(jnp.take(omega.reshape(LEAF_DEV, LEAF_PTS, columns), send, axis=0), "leaf", 0, 0, tiled=True)
    mine = lax.dynamic_index_in_dim(tree, me, 0, keepdims=False)
    smaller = jnp.any(jnp.logical_and((mine[:, None] >> 2) == (mine[None, :] >> 2), mine[None, :] < mine[:, None]), axis=1)
    arrival = ((mine >> 2) * SLOTS + smaller.astype(jnp.int32)).reshape(LEAF_DEV, NEAR)

    def one(member):
        slots = lax.dynamic_index_in_dim(arrival, member, 0, keepdims=False)
        far = jnp.moveaxis(jnp.take(got_points, slots, axis=0), 0, 1).reshape(DIMS, NEAR * LEAF_PTS)
        samples = jnp.take(got_samples, slots, axis=0).reshape(NEAR * LEAF_PTS, columns)
        own = lax.dynamic_index_in_dim(leaf_points, member, 0, keepdims=False)
        return jnp.dot(kernel_tile(own, far), samples, preferred_element_type=F32)

    return lax.map(one, jnp.arange(LEAF_DEV, dtype=jnp.int32))


def call(kernel, out_shape, in_specs, out_specs, **more):
    return pl.pallas_call(
        kernel,
        out_shape=out_shape,
        in_specs=in_specs,
        out_specs=out_specs,
        compiler_params=pltpu.CompilerParams(vmem_limit_bytes=VMEM_LIMIT),
        **more,
    )


def shards(points, omega, near_lists, leaf_order, pivots):
    columns = omega.shape[1]
    near = near_lists.T
    leaves = omega.reshape(LEAF_DEV, LEAF_PTS, columns)
    shape = jax.ShapeDtypeStruct
    block = shape((LEAF_PTS, columns), BF16)
    smem = pl.BlockSpec(memory_space=SMEM)
    anywhere = pl.BlockSpec(memory_space=pl.ANY)
    pack_shape = shape((SLOTS, PACK, columns), BF16)
    table, *packs = call(
        send_kernel, [shape((T_LEN,), jnp.int32)] + [pack_shape] * BESIDE, [smem, smem] + vm(4), [smem] + vm(BESIDE)
    )(near, leaf_order, near, leaf_order.reshape(-1, 128), points, leaves)

    total_shape = shape((LEAF_DEV, LEAF_PTS, columns), F32)
    coupling_shape = shape((LEAF_DEV * SKEL, LEAF_DEV * SKEL), BF16)

    def shift(value, k):
        return lax.ppermute(value, "samp", [(s, (s + k) % 4) for s in range(4)])

    def turned(values):
        moved = {}
        for k in range(1, 4):
            moved[k] = shift(values[k], k)
        return [moved[k] for k in range(1, 4)]

    def near_branch(points, leaves, near_lists, leaf_order, pivots, table, packs):
        def move(pack, offset):
            return lax.ppermute(pack, "leaf", [((n + offset[n % 2]) % NODES, n) for n in range(NODES)])

        arrived = []
        for i in range(BESIDE):
            arrived.append(move(packs[i], OFFSETS[i]))
        total, left = call(
            own_kernel, [total_shape, shape((LEAF_DEV * LEAF_PTS, AUG), BF16)], [smem] + vm(2), vm(2)
        )(table, points, leaves)
        skeleton, beside, half = call(
            half_kernel,
            [shape((DIMS, LEAF_DEV * SKEL), BF16), shape((SLOTS, PACK + SLOTS * DIMS, columns), BF16), pack_shape],
            [smem] + vm(3) + [anywhere] * 2,
            vm(3),
        )(table, points, leaves, pivots, left, arrived[0])
        arrived.append(move(beside, OFFSETS[BESIDE]))
        arrived.append(move(half, OFFSETS[HALF]))
        first, second, last = GROUPS
        (total,) = call(
            functools.partial(early_kernel, first), [total_shape], [smem] + vm(2 + len(first)), vm(1)
        )(table, left, total, *[arrived[i] for i in first])
        total, coupling = call(
            functools.partial(couple_kernel, second), [total_shape, coupling_shape], [smem] + vm(4 + len(second)), vm(2)
        )(table, left, total, skeleton, arrived[BESIDE], *[arrived[i] for i in second])
        total, *blocks = call(
            functools.partial(late_kernel, last), [total_shape] + [block] * 4, [smem] + vm(2 + len(last)), vm(5)
        )(table, left, total, *[arrived[i] for i in last])
        return total, blocks, coupling

    def any_branch(points, leaves, near_lists, leaf_order, pivots, table, packs):
        total = general_sample(points, leaves.reshape(-1, columns), near_lists, leaf_order)
        column = lax.axis_index("samp")
        blocks = [lax.dynamic_index_in_dim(total, (column + k) & 3, 0, keepdims=False).astype(BF16) for k in range(4)]
        skeleton = jnp.take_along_axis(points.reshape(DIMS, LEAF_DEV, LEAF_PTS), pivots[None], axis=2)
        skeleton = skeleton.reshape(DIMS, LEAF_DEV * SKEL)
        return total, blocks, kernel_tile(skeleton, lax.ppermute(skeleton, "leaf", [(n, n ^ 1) for n in range(NODES)]))

    total, blocks, coupling = lax.cond(
        table[T_OK] > 0, near_branch, any_branch, points, leaves, near_lists, leaf_order, pivots, table, packs
    )
    swapped = [blocks[0]] + turned(blocks)
    (rows,) = call(rows_kernel, [shape((LEAF_DEV * SKEL, columns), F32)], vm(2), vm(1))(total, pivots)
    (interpolation,) = call(
        solve_kernel, [shape((LEAF_PTS, SKEL), BF16)], vm(5) + [anywhere], vm(1)
    )(*swapped, pivots, rows)
    spread = [interpolation] + turned([interpolation] * 4)
    projected_shape = [shape((LEAF_DEV * SKEL, columns), BF16)]
    (projected,) = call(functools.partial(project_kernel, FIRST), projected_shape, vm(1 + len(FIRST)), vm(1))(
        leaves, *[spread[k] for k in FIRST]
    )
    (projected,) = call(functools.partial(project_kernel, SECOND), projected_shape, vm(2 + len(SECOND)), vm(1))(
        leaves, projected, *[spread[k] for k in SECOND]
    )
    crossed = lax.ppermute(projected, "leaf", [(n, n ^ 1) for n in range(NODES)])
    (stacked,) = call(stack_kernel, [shape((LEAF_DEV * LEAF_PTS, SKEL), BF16)], vm(4), vm(1))(*spread)
    (parent,) = call(parent_kernel, [shape((LEAF_DEV * SKEL, columns), F32)], vm(3), vm(1))(rows, coupling, crossed)
    return stacked, parent


def solution(mesh):
    placed = (P(None, "leaf"), P("leaf", "samp"), P(), P(), P("leaf", None))
    return jax.shard_map(
        shards,
        mesh=mesh,
        in_specs=placed,
        out_specs=(P("leaf", None), P("leaf", "samp")),
        check_vma=False,
    )
```

profile of v0, /device:TPU:123, one launch (start us, length us, event | category | flops | bytes accessed | tf_op | source)
XLA Modules:
  0.0 82.6 jit_solution(10432221452160219318)
XLA Ops:
  0.6 2.4 %shard_map.68 = (s32[128]{0:T(128)S(1)}, bf16[2,544,128]{2,1,0:T(8,128)(2,1)S(1)}, bf16[2,544,128]{2,1,0:T(8,128)(2,1)}, bf16[2,544,128]{2,1,0:T(8,128)(2,1)}, bf16[2,544,128]{2,1,0:T(8,128)(2,1)}) custom-call(s32[8,256]{1,0:T(8,128)} %bitcast.118, s32[256]{0:T(256)} %order_s.1, s32[8,256]{1,0:T(8,128)} %bitcast.119, s32[2,128]{1,0:T(2,128)} %bitcast.104, ...), custom_call_target="tpu_custom_call" | custom-call | tf_op jit(solution)/shard_map/pallas_call | solution.py:373
  3.1 52.0 %conditional.1 = (f32[4,512,128]{2,1,0:T(8,128)}, bf16[512,128]{1,0:T(8,128)(2,1)S(1)}, bf16[512,128]{1,0:T(8,128)(2,1)S(1)}, bf16[512,128]{1,0:T(8,128)(2,1)S(1...) conditional(s32[]{:T(128)} %bitcast.33, (s32[256,8]{0,1:T(8,128)}, s32[256]{0:T(256)}, ...), branch_computations={%region_0.11_spmd, %region_11.12_spmd} | conditional | flops 596083072 | bytes 137072240 | solution.py:427
  3.4 2.6 %collective-permute-start = (bf16[2,544,128]{2,1,0:T(8,128)(2,1)S(1)}, bf16[2,544,128]{2,1,0:T(8,128)(2,1)S(1)}, u32[]{:S(2)}, u32[]{:S(2)}) collective-permute-start(bf16[2,544,128]{2,1,0:T(8,128)(2,1)S(1)} %get-tuple-element.76), channel_id=1, source_target_pairs={{248,0},{252,4},{0,8},{4,12},{8,16},{12,20},{16,24},{20,28},{24,32... | collective-permute-start | bytes 835592 | tf_op jit(solution)/shard_map/cond/branch_1_fun/ppermute | solution.py:391
  6.0 4.1 %branch_1_fun.5 = (f32[4,512,128]{2,1,0:T(8,128)S(1)}, bf16[2048,16]{1,0:T(8,128)(2,1)S(1)}) custom-call(s32[128]{0:T(128)S(1)} %get-tuple-element.70.table, bf16[8,2048]{1,0:T(8,128)(2,1)} %get-tuple-element.71.points, bf16[4,512,128]{2,1,0:T(8,128)(2,1)} %get-tuple-element.72.omega), custom_call_target="tpu_custom_call" | custom-call | tf_op jit(solution)/shard_map/cond/branch_1_fun/pallas_call | solution.py:396
  11.3 1.3 %branch_1_fun.6 = (bf16[8,512]{1,0:T(8,128)(2,1)S(1)}, bf16[2,560,128]{2,1,0:T(8,128)(2,1)S(1)}, bf16[2,544,128]{2,1,0:T(8,128)(2,1)S(1)}) custom-call(s32[128]{0:T(128)S(1)} %get-tuple-element.70.table, bf16[8,2048]{1,0:T(8,128)(2,1)} %get-tuple-element.71.points, bf16[4,512,128]{2,1,0:T(8,128)(2,1)} %get-tuple-element.72.omega, ...), custom_call_target="tpu_custom_call" | custom-call | tf_op jit(solution)/shard_map/cond/branch_1_fun/pallas_call | solution.py:399
  12.6 1.6 %collective-permute-start.1 = (bf16[2,560,128]{2,1,0:T(8,128)(2,1)S(1)}, bf16[2,560,128]{2,1,0:T(8,128)(2,1)S(1)}, u32[]{:S(2)}, u32[]{:S(2)}) collective-permute-start(bf16[2,560,128]{2,1,0:T(8,128)(2,1)S(1)} %get-tuple-element.77), channel_id=1, source_target_pairs={{4,0},{0,4},{12,8},{8,12},{20,16},{16,20},{28,24},{24,28},{36,32},... | collective-permute-start | bytes 860168 | tf_op jit(solution)/shard_map/cond/branch_1_fun/ppermute | solution.py:391
  14.2 5.5 %collective-permute-start.2 = (bf16[2,544,128]{2,1,0:T(8,128)(2,1)}, bf16[2,544,128]{2,1,0:T(8,128)(2,1)S(1)}, u32[]{:S(2)}, u32[]{:S(2)}) collective-permute-start(bf16[2,544,128]{2,1,0:T(8,128)(2,1)} %get-tuple-element.78), channel_id=1, source_target_pairs={{252,0},{248,4},{4,8},{0,12},{12,16},{8,20},{20,24},{16,28},{28,32... | collective-permute-start | bytes 835592 | tf_op jit(solution)/shard_map/cond/branch_1_fun/ppermute | solution.py:391
  19.7 1.6 %collective-permute-start.4 = (bf16[2,544,128]{2,1,0:T(8,128)(2,1)}, bf16[2,544,128]{2,1,0:T(8,128)(2,1)S(1)}, u32[]{:S(2)}, u32[]{:S(2)}) collective-permute-start(bf16[2,544,128]{2,1,0:T(8,128)(2,1)} %get-tuple-element.81), channel_id=1, source_target_pairs={{244,0},{8,4},{252,8},{16,12},{4,16},{24,20},{12,24},{32,28},{20,3... | collective-permute-start | bytes 835592 | tf_op jit(solution)/shard_map/cond/branch_1_fun/ppermute | solution.py:391
  21.2 1.7 %collective-permute-start.5 = (bf16[2,544,128]{2,1,0:T(8,128)(2,1)S(1)}, bf16[2,544,128]{2,1,0:T(8,128)(2,1)S(1)}, u32[]{:S(2)}, u32[]{:S(2)}) collective-permute-start(bf16[2,544,128]{2,1,0:T(8,128)(2,1)S(1)} %get-tuple-element.83), channel_id=1, source_target_pairs={{128,0},{132,4},{136,8},{140,12},{144,16},{148,20},{152,24},{156,2... | collective-permute-start | bytes 835592 | tf_op jit(solution)/shard_map/cond/branch_1_fun/ppermute | solution.py:391
  22.9 8.4 %collective-permute-done.2.rest_2_ = bf16[2,544,128]{2,1,0:T(8,128)(2,1)S(1)} collective-permute-done((bf16[2,544,128]{2,1,0:T(8,128)(2,1)}, bf16[2,544,128]{2,1,0:T(8,128)(2,1)S(1)}, u32[]{:S(2)}, u32[]{:S(2)}) %collective-permute-start.2) | collective-permute-done | bytes 278560 | tf_op jit(solution)/shard_map/cond/branch_1_fun/ppermute | solution.py:391
  31.4 6.3 %branch_1_fun.7.before = f32[4,512,128]{2,1,0:T(8,128)S(1)} custom-call(s32[128]{0:T(128)S(1)} %get-tuple-element.70.table, bf16[2048,16]{1,0:T(8,128)(2,1)S(1)} %get-tuple-element.73.left, f32[4,512,128]{2,1,0:T(8,128)S(1)} %get-tuple-element.74.before, bf16[2,560,128]{2,1,0:T(8,128)(2,1)S(1)} %collective-permute-done.1.rest_0_.beside, ...), custom_call_target="tpu_custom_call" | custom-call | tf_op jit(solution)/shard_map/cond/branch_1_fun/pallas_call | solution.py:408
  37.7 9.1 %collective-permute-done.4.rest_1_ = bf16[2,544,128]{2,1,0:T(8,128)(2,1)S(1)} collective-permute-done((bf16[2,544,128]{2,1,0:T(8,128)(2,1)}, bf16[2,544,128]{2,1,0:T(8,128)(2,1)S(1)}, u32[]{:S(2)}, u32[]{:S(2)}) %collective-permute-start.4) | collective-permute-done | bytes 278560 | tf_op jit(solution)/shard_map/cond/branch_1_fun/ppermute | solution.py:391
  46.8 5.3 %branch_1_fun.8 = (f32[4,512,128]{2,1,0:T(8,128)S(1)}, bf16[512,512]{1,0:T(8,128)(2,1)S(1)}) custom-call(s32[128]{0:T(128)S(1)} %get-tuple-element.70.table, bf16[2048,16]{1,0:T(8,128)(2,1)S(1)} %get-tuple-element.73.left, f32[4,512,128]{2,1,0:T(8,128)S(1)} %branch_1_fun.7.before, bf16[8,512]{1,0:T(8,128)(2,1)S(1)} %get-tuple-element.79.skeleton, ...), custom_call_target="tpu_custom_call" | custom-call | tf_op jit(solution)/shard_map/cond/branch_1_fun/pallas_call | solution.py:411
  52.2 3.0 %branch_1_fun.9 = (f32[4,512,128]{2,1,0:T(8,128)}, bf16[512,128]{1,0:T(8,128)(2,1)S(1)}, bf16[512,128]{1,0:T(8,128)(2,1)S(1)}, bf16[512,128]{1,0:T(8,128)(2,1)S(1)}, bf16[512,128]{1,0:T(8,128)(2,1)S(1)}) custom-call(s32[128]{0:T(128)S(1)} %get-tuple-element.70.table, bf16[2048,16]{1,0:T(8,128)(2,1)S(1)} %get-tuple-element.73.left, ...), custom_call_target="tpu_custom_call" | custom-call | tf_op jit(solution)/shard_map/cond/branch_1_fun/pallas_call | solution.py:414
  57.2 1.9 %collective-permute-start.9 = (bf16[512,128]{1,0:T(8,128)(2,1)S(1)}, bf16[512,128]{1,0:T(8,128)(2,1)S(1)}, u32[]{:S(2)}, u32[]{:S(2)}) collective-permute-start(bf16[512,128]{1,0:T(8,128)(2,1)S(1)} %get-tuple-element.111), channel_id=1, source_target_pairs={{0,3},{1,0},{2,1},{3,2},{4,7},{5,4},{6,5},{7,6},{8,11},{9,8},{10,9... | collective-permute-start | bytes 393224 | tf_op jit(solution)/shard_map/ppermute | solution.py:381
  59.1 2.3 %shard_map.69.rows = f32[512,128]{1,0:T(8,128)S(1)} custom-call(f32[4,512,128]{2,1,0:T(8,128)} %get-tuple-element.112.total, s32[4,128]{1,0:T(4,128)} %pivots.3), custom_call_target="tpu_custom_call" | custom-call | tf_op jit(solution)/shard_map/pallas_call | solution.py:431
  61.4 1.3 %collective-permute-done.8.b2 = bf16[512,128]{1,0:T(8,128)(2,1)S(1)} collective-permute-done((bf16[512,128]{1,0:T(8,128)(2,1)S(1)}, bf16[512,128]{1,0:T(8,128)(2,1)S(1)}, u32[]{:S(2)}, u32[]{:S(2)}) %collective-permute-start.8) | collective-permute-done | bytes 131104 | tf_op jit(solution)/shard_map/ppermute | solution.py:381
  62.7 2.1 %collective-permute-done.9.b3 = bf16[512,128]{1,0:T(8,128)(2,1)S(1)} collective-permute-done((bf16[512,128]{1,0:T(8,128)(2,1)S(1)}, bf16[512,128]{1,0:T(8,128)(2,1)S(1)}, u32[]{:S(2)}, u32[]{:S(2)}) %collective-permute-start.9) | collective-permute-done | bytes 131104 | tf_op jit(solution)/shard_map/ppermute | solution.py:381
  64.8 4.1 %shard_map.70.i0.rest_0_ = bf16[512,128]{1,0:T(8,128)(2,1)S(1)} custom-call(bf16[512,128]{1,0:T(8,128)(2,1)S(1)} %get-tuple-element.108.b0, bf16[512,128]{1,0:T(8,128)(2,1)S(1)} %collective-permute-done.7.b1, bf16[512,128]{1,0:T(8,128)(2,1)S(1)} %collective-permute-done.8.b2, bf16[512,128]{1,0:T(8,128)(2,1)S(1)} %collective-permute-done.9.b3, ...), custom_call_target="tpu_custom_call" | custom-call | tf_op jit(solution)/shard_map/pallas_call | solution.py:432
  70.0 1.5 %collective-permute-start.11 = (bf16[512,128]{1,0:T(8,128)(2,1)S(1)}, bf16[512,128]{1,0:T(8,128)(2,1)S(1)}, u32[]{:S(2)}, u32[]{:S(2)}) collective-permute-start(bf16[512,128]{1,0:T(8,128)(2,1)S(1)} %shard_map.70.i0.rest_0_), channel_id=1, source_target_pairs={{0,2},{1,3},{2,0},{3,1},{4,6},{5,7},{6,4},{7,5},{8,10},{9,11},{10,... | collective-permute-start | bytes 393224 | tf_op jit(solution)/shard_map/ppermute | solution.py:381
  71.5 1.4 %collective-permute-start.12 = (bf16[512,128]{1,0:T(8,128)(2,1)S(1)}, bf16[512,128]{1,0:T(8,128)(2,1)S(1)}, u32[]{:S(2)}, u32[]{:S(2)}) collective-permute-start(bf16[512,128]{1,0:T(8,128)(2,1)S(1)} %shard_map.70.i0.rest_0_), channel_id=1, source_target_pairs={{0,3},{1,0},{2,1},{3,2},{4,7},{5,4},{6,5},{7,6},{8,11},{9,8},{10,9... | collective-permute-start | bytes 393224 | tf_op jit(solution)/shard_map/ppermute | solution.py:381
  73.0 1.3 %shard_map.72.rest_0_ = bf16[512,128]{1,0:T(8,128)(2,1)S(1)} custom-call(bf16[4,512,128]{2,1,0:T(8,128)(2,1)} %bitcast.107, bf16[512,128]{1,0:T(8,128)(2,1)S(1)} %shard_map.70.i0.rest_0_), custom_call_target="tpu_custom_call" | custom-call | tf_op jit(solution)/shard_map/pallas_call | solution.py:437
  74.2 1.2 %collective-permute-done.11.i2.rest_2_ = bf16[512,128]{1,0:T(8,128)(2,1)S(1)} collective-permute-done((bf16[512,128]{1,0:T(8,128)(2,1)S(1)}, bf16[512,128]{1,0:T(8,128)(2,1)S(1)}, u32[]{:S(2)}, u32[]{:S(2)}) %collective-permute-start.11) | collective-permute-done | bytes 131104 | tf_op jit(solution)/shard_map/ppermute | solution.py:381
  75.5 3.9 %collective-permute-done.12.i3.rest_3_ = bf16[512,128]{1,0:T(8,128)(2,1)S(1)} collective-permute-done((bf16[512,128]{1,0:T(8,128)(2,1)S(1)}, bf16[512,128]{1,0:T(8,128)(2,1)S(1)}, u32[]{:S(2)}, u32[]{:S(2)}) %collective-permute-start.12) | collective-permute-done | bytes 131104 | tf_op jit(solution)/shard_map/ppermute | solution.py:381
  (19 shorter events, 7.7 us)
Async XLA Ops:
  3.1 61.7 %copy-start.4 = (s32[4,128]{1,0:T(4,128)S(1)}, s32[4,128]{1,0:T(4,128)}, u32[]{:S(2)}) copy-start(s32[4,128]{1,0:T(4,128)} %pivots.3) | copy-start | bytes 6148
  3.1 76.3 %copy-start.1 = (bf16[2048,128]{1,0:T(8,128)(2,1)S(1)}, bf16[2048,128]{1,0:T(8,128)(2,1)}, u32[]{:S(2)}) copy-start(bf16[2048,128]{1,0:T(8,128)(2,1)} %param.10) | copy-start | bytes 1572868
  3.4 7.9 %collective-permute-start = (bf16[2,544,128]{2,1,0:T(8,128)(2,1)S(1)}, bf16[2,544,128]{2,1,0:T(8,128)(2,1)S(1)}, u32[]{:S(2)}, u32[]{:S(2)}) collective-permute-start(bf16[2,544,128]{2,1,0:T(8,128)(2,1)S(1)} %get-tuple-element.76), channel_id=1, source_target_pairs={{248,0},{252,4},{0,8},{4,12},{8,16},{12,20},{16,24},{20,28},{24,32... | collective-permute-start | bytes 835592 | tf_op jit(solution)/shard_map/cond/branch_1_fun/ppermute | solution.py:391
  12.6 18.8 %collective-permute-start.1 = (bf16[2,560,128]{2,1,0:T(8,128)(2,1)S(1)}, bf16[2,560,128]{2,1,0:T(8,128)(2,1)S(1)}, u32[]{:S(2)}, u32[]{:S(2)}) collective-permute-start(bf16[2,560,128]{2,1,0:T(8,128)(2,1)S(1)} %get-tuple-element.77), channel_id=1, source_target_pairs={{4,0},{0,4},{12,8},{8,12},{20,16},{16,20},{28,24},{24,28},{36,32},... | collective-permute-start | bytes 860168 | tf_op jit(solution)/shard_map/cond/branch_1_fun/ppermute | solution.py:391
  14.2 17.2 %collective-permute-start.2 = (bf16[2,544,128]{2,1,0:T(8,128)(2,1)}, bf16[2,544,128]{2,1,0:T(8,128)(2,1)S(1)}, u32[]{:S(2)}, u32[]{:S(2)}) collective-permute-start(bf16[2,544,128]{2,1,0:T(8,128)(2,1)} %get-tuple-element.78), channel_id=1, source_target_pairs={{252,0},{248,4},{4,8},{0,12},{12,16},{8,20},{20,24},{16,28},{28,32... | collective-permute-start | bytes 835592 | tf_op jit(solution)/shard_map/cond/branch_1_fun/ppermute | solution.py:391
  19.7 18.1 %collective-permute-start.3 = (bf16[2,544,128]{2,1,0:T(8,128)(2,1)}, bf16[2,544,128]{2,1,0:T(8,128)(2,1)S(1)}, u32[]{:S(2)}, u32[]{:S(2)}) collective-permute-start(bf16[2,544,128]{2,1,0:T(8,128)(2,1)} %get-tuple-element.80), channel_id=1, source_target_pairs={{8,0},{12,4},{16,8},{20,12},{24,16},{28,20},{32,24},{36,28},{40,32... | collective-permute-start | bytes 835592 | tf_op jit(solution)/shard_map/cond/branch_1_fun/ppermute | solution.py:391
  19.7 27.2 %collective-permute-start.4 = (bf16[2,544,128]{2,1,0:T(8,128)(2,1)}, bf16[2,544,128]{2,1,0:T(8,128)(2,1)S(1)}, u32[]{:S(2)}, u32[]{:S(2)}) collective-permute-start(bf16[2,544,128]{2,1,0:T(8,128)(2,1)} %get-tuple-element.81), channel_id=1, source_target_pairs={{244,0},{8,4},{252,8},{16,12},{4,16},{24,20},{12,24},{32,28},{20,3... | collective-permute-start | bytes 835592 | tf_op jit(solution)/shard_map/cond/branch_1_fun/ppermute | solution.py:391
  21.2 30.9 %collective-permute-start.5 = (bf16[2,544,128]{2,1,0:T(8,128)(2,1)S(1)}, bf16[2,544,128]{2,1,0:T(8,128)(2,1)S(1)}, u32[]{:S(2)}, u32[]{:S(2)}) collective-permute-start(bf16[2,544,128]{2,1,0:T(8,128)(2,1)S(1)} %get-tuple-element.83), channel_id=1, source_target_pairs={{128,0},{132,4},{136,8},{140,12},{144,16},{148,20},{152,24},{156,2... | collective-permute-start | bytes 835592 | tf_op jit(solution)/shard_map/cond/branch_1_fun/ppermute | solution.py:391
  55.2 6.3 %collective-permute-start.7 = (bf16[512,128]{1,0:T(8,128)(2,1)S(1)}, bf16[512,128]{1,0:T(8,128)(2,1)S(1)}, u32[]{:S(2)}, u32[]{:S(2)}) collective-permute-start(bf16[512,128]{1,0:T(8,128)(2,1)S(1)} %get-tuple-element.109), channel_id=1, source_target_pairs={{0,1},{1,2},{2,3},{3,0},{4,5},{5,6},{6,7},{7,4},{8,9},{9,10},{10,1... | collective-permute-start | bytes 393224 | tf_op jit(solution)/shard_map/ppermute | solution.py:381
  56.4 6.3 %collective-permute-start.8 = (bf16[512,128]{1,0:T(8,128)(2,1)S(1)}, bf16[512,128]{1,0:T(8,128)(2,1)S(1)}, u32[]{:S(2)}, u32[]{:S(2)}) collective-permute-start(bf16[512,128]{1,0:T(8,128)(2,1)S(1)} %get-tuple-element.110), channel_id=1, source_target_pairs={{0,2},{1,3},{2,0},{3,1},{4,6},{5,7},{6,4},{7,5},{8,10},{9,11},{10,... | collective-permute-start | bytes 393224 | tf_op jit(solution)/shard_map/ppermute | solution.py:381
  57.2 7.6 %collective-permute-start.9 = (bf16[512,128]{1,0:T(8,128)(2,1)S(1)}, bf16[512,128]{1,0:T(8,128)(2,1)S(1)}, u32[]{:S(2)}, u32[]{:S(2)}) collective-permute-start(bf16[512,128]{1,0:T(8,128)(2,1)S(1)} %get-tuple-element.111), channel_id=1, source_target_pairs={{0,3},{1,0},{2,1},{3,2},{4,7},{5,4},{6,5},{7,6},{8,11},{9,8},{10,9... | collective-permute-start | bytes 393224 | tf_op jit(solution)/shard_map/ppermute | solution.py:381
  68.9 5.3 %collective-permute-start.10 = (bf16[512,128]{1,0:T(8,128)(2,1)S(1)}, bf16[512,128]{1,0:T(8,128)(2,1)S(1)}, u32[]{:S(2)}, u32[]{:S(2)}) collective-permute-start(bf16[512,128]{1,0:T(8,128)(2,1)S(1)} %shard_map.70.i0.rest_0_), channel_id=1, source_target_pairs={{0,1},{1,2},{2,3},{3,0},{4,5},{5,6},{6,7},{7,4},{8,9},{9,10},{10,1... | collective-permute-start | bytes 393224 | tf_op jit(solution)/shard_map/ppermute | solution.py:381
  70.0 5.4 %collective-permute-start.11 = (bf16[512,128]{1,0:T(8,128)(2,1)S(1)}, bf16[512,128]{1,0:T(8,128)(2,1)S(1)}, u32[]{:S(2)}, u32[]{:S(2)}) collective-permute-start(bf16[512,128]{1,0:T(8,128)(2,1)S(1)} %shard_map.70.i0.rest_0_), channel_id=1, source_target_pairs={{0,2},{1,3},{2,0},{3,1},{4,6},{5,7},{6,4},{7,5},{8,10},{9,11},{10,... | collective-permute-start | bytes 393224 | tf_op jit(solution)/shard_map/ppermute | solution.py:381
  71.5 7.9 %collective-permute-start.12 = (bf16[512,128]{1,0:T(8,128)(2,1)S(1)}, bf16[512,128]{1,0:T(8,128)(2,1)S(1)}, u32[]{:S(2)}, u32[]{:S(2)}) collective-permute-start(bf16[512,128]{1,0:T(8,128)(2,1)S(1)} %shard_map.70.i0.rest_0_), channel_id=1, source_target_pairs={{0,3},{1,0},{2,1},{3,2},{4,7},{5,4},{6,5},{7,6},{8,11},{9,8},{10,9... | collective-permute-start | bytes 393224 | tf_op jit(solution)/shard_map/ppermute | solution.py:381
  79.7 1.9 %collective-permute-start.13 = (bf16[512,128]{1,0:T(8,128)(2,1)S(1)}, bf16[512,128]{1,0:T(8,128)(2,1)S(1)}, u32[]{:S(2)}, u32[]{:S(2)}) collective-permute-start(bf16[512,128]{1,0:T(8,128)(2,1)S(1)} %shard_map.73), channel_id=1, source_target_pairs={{0,4},{4,0},{8,12},{12,8},{16,20},{20,16},{24,28},{28,24},{32,36},... | collective-permute-start | bytes 393224 | tf_op jit(solution)/shard_map/ppermute | solution.py:443
where the time goes:
time: 82.8 us; the launch traced here: 82.6 us
  Pallas kernels  32.4 us (39%)
  waiting for transfers between devices  27.4 us (33%)
  starting transfers between devices  21.8 us (26%)
    ppermute x6, waiting for transfers between devices, move(): lax.ppermute(pack, 'leaf', [((n + offset[n % 2]) % NODES, n) for n in ran...  18.8 us
    ppermute x6, starting transfers between devices, move(): lax.ppermute(pack, 'leaf', [((n + offset[n % 2]) % NODES, n) for n in ran...  13 us
    ppermute x6, waiting for transfers between devices, shift(): return lax.ppermute(value, 'samp', [(s, (s + k) % 4) for s in range(4)])  8.47 us
    ppermute x6, starting transfers between devices, shift(): return lax.ppermute(value, 'samp', [(s, (s + k) % 4) for s in range(4)])  7.95 us
    pallas_call x1, Pallas kernels, near_branch(): call(functools.partial(early_kernel, first), [total_shape], [smem] + vm(2...  6.35 us
    pallas_call x1, Pallas kernels, near_branch(): call(functools.partial(couple_kernel, second), [total_shape, coupling_sha...  5.31 us
    pallas_call x1, Pallas kernels, shards(): call(solve_kernel, [shape((LEAF_PTS, SKEL), BF16)], vm(5) + [anywhere], v...  4.15 us
    pallas_call x1, Pallas kernels, near_branch(): call(own_kernel, [total_shape, shape((LEAF_DEV * LEAF_PTS, AUG), BF16)],...  4.11 us
  transfers between devices with their start and end apart: 13, of which 8 were waited for; matrix products, arithmetic and copies ran while one was open for 0% of the time, Pallas kernels for 24%

commit v1 on v0

--- a/solution.py
+++ b/solution.py
@@ -229,20 +229,25 @@
 
 
 def late_kernel(group, table, left, before, *rest):
-    packs, (total, *blocks) = rest[:len(group)], rest[len(group):]
+    packs, (low, *blocks, total) = rest[:len(group)], rest[len(group):]
     total[...] = before[...]
     add_packs(group, table, left, packs, total)
     column = lax.axis_index("samp")
     for step in range(4):
-        blocks[step][...] = total[(column + step) & 3].astype(BF16)
-
-
-def rows_kernel(total, pivots, rows):
-    for member in range(LEAF_DEV):
-        chosen = lax.broadcasted_iota(jnp.int32, (LEAF_PTS, SKEL), 0) == pivots[member:member + 1, :]
-        pick = jnp.where(chosen, 1.0, 0.0)
-        values = total[member]
-        rows[member * SKEL:(member + 1) * SKEL, :] = lax.dot_general(pick, values, (((0,), (0,)), ((), ())), preferred_element_type=F32, precision=HIGHEST)
+        values = total[(column + step) & 3]
+        high = values.astype(BF16)
+        blocks[step][...] = high
+        low[step] = (values - high.astype(F32)).astype(BF16)
+
+
+def rows_kernel(low, b0, b1, b2, b3, pivots, rows):
+    column = lax.axis_index("samp")
+    for step, block in enumerate((b0, b1, b2, b3)):
+        member = (column + step) & 3
+        chosen = lax.broadcasted_iota(jnp.int32, (LEAF_PTS, SKEL), 0) == pivots[pl.ds(member, 1), :]
+        pick = jnp.where(chosen, 1.0, 0.0).astype(BF16)
+        spot = pl.ds(pl.multiple_of(member * SKEL, SKEL), SKEL)
+        rows[spot, :] = dot_tn(pick, block[...]) + dot_tn(pick, low[step])
 
 
 def matmul3(a, b):
@@ -375,6 +380,7 @@
     )(near, leaf_order, near, leaf_order.reshape(-1, 128), points, leaves)
 
     total_shape = shape((LEAF_DEV, LEAF_PTS, columns), F32)
+    low_shape = shape((LEAF_DEV, LEAF_PTS, columns), BF16)
     coupling_shape = shape((LEAF_DEV * SKEL, LEAF_DEV * SKEL), BF16)
 
     def shift(value, k):
@@ -411,24 +417,30 @@
         total, coupling = call(
             functools.partial(couple_kernel, second), [total_shape, coupling_shape], [smem] + vm(4 + len(second)), vm(2)
         )(table, left, total, skeleton, arrived[BESIDE], *[arrived[i] for i in second])
-        total, *blocks = call(
-            functools.partial(late_kernel, last), [total_shape] + [block] * 4, [smem] + vm(2 + len(last)), vm(5)
+        low, *blocks = call(
+            functools.partial(late_kernel, last),
+            [low_shape] + [block] * 4,
+            [smem] + vm(2 + len(last)),
+            vm(5),
+            scratch_shapes=[pltpu.VMEM(total_shape.shape, F32)],
         )(table, left, total, *[arrived[i] for i in last])
-        return total, blocks, coupling
+        return low, blocks, coupling
 
     def any_branch(points, leaves, near_lists, leaf_order, pivots, table, packs):
         total = general_sample(points, leaves.reshape(-1, columns), near_lists, leaf_order)
         column = lax.axis_index("samp")
-        blocks = [lax.dynamic_index_in_dim(total, (column + k) & 3, 0, keepdims=False).astype(BF16) for k in range(4)]
+        turned_total = [lax.dynamic_index_in_dim(total, (column + k) & 3, 0, keepdims=False) for k in range(4)]
+        blocks = [value.astype(BF16) for value in turned_total]
+        low = jnp.stack([(v - h.astype(F32)).astype(BF16) for v, h in zip(turned_total, blocks)])
         skeleton = jnp.take_along_axis(points.reshape(DIMS, LEAF_DEV, LEAF_PTS), pivots[None], axis=2)
         skeleton = skeleton.reshape(DIMS, LEAF_DEV * SKEL)
-        return total, blocks, kernel_tile(skeleton, lax.ppermute(skeleton, "leaf", [(n, n ^ 1) for n in range(NODES)]))
-
-    total, blocks, coupling = lax.cond(
+        return low, blocks, kernel_tile(skeleton, lax.ppermute(skeleton, "leaf", [(n, n ^ 1) for n in range(NODES)]))
+
+    low, blocks, coupling = lax.cond(
         table[T_OK] > 0, near_branch, any_branch, points, leaves, near_lists, leaf_order, pivots, table, packs
     )
     swapped = [blocks[0]] + turned(blocks)
-    (rows,) = call(rows_kernel, [shape((LEAF_DEV * SKEL, columns), F32)], vm(2), vm(1))(total, pivots)
+    (rows,) = call(rows_kernel, [shape((LEAF_DEV * SKEL, columns), F32)], vm(6), vm(1))(low, *blocks, pivots)
     (interpolation,) = call(
         solve_kernel, [shape((LEAF_PTS, SKEL), BF16)], vm(5) + [anywhere], vm(1)
     )(*swapped, pivots, rows)

time: 82.8 us -> 82.3 us (level)
  Pallas kernels: 32.4 us -> 30.3 us
  waiting for transfers between devices: 27.4 us -> 28.5 us
    pallas_call x2, Pallas kernels: 5.33 us -> 3.31 us  [the longest x1 2.14 us: near_branch(): call(functools.partial(late_kernel, last), [low_shape] + [block] * 4, [sm...]
    ppermute x6, waiting for transfers between devices: 8.47 us -> 9.62 us  [shift(): return lax.ppermute(value, 'samp', [(s, (s + k) % 4) for s in range(4)])]
  transfers between devices with their start and end apart: 13 -> 13, of which waited for: 8 -> 8; matrix products, arithmetic and copies ran while one was open for 0% -> 0% of each run, Pallas kernels for 24% -> 23%
where the time goes in v1:
time: 82.3 us; the launch traced here: 82.1 us
  Pallas kernels  30.3 us (37%)
  waiting for transfers between devices  28.5 us (35%)
  starting transfers between devices  22.2 us (27%)
    ppermute x6, waiting for transfers between devices, move(): lax.ppermute(pack, 'leaf', [((n + offset[n % 2]) % NODES, n) for n in ran...  18.8 us
    ppermute x6, starting transfers between devices, move(): lax.ppermute(pack, 'leaf', [((n + offset[n % 2]) % NODES, n) for n in ran...  13 us
    ppermute x6, waiting for transfers between devices, shift(): return lax.ppermute(value, 'samp', [(s, (s + k) % 4) for s in range(4)])  9.62 us
    ppermute x6, starting transfers between devices, shift(): return lax.ppermute(value, 'samp', [(s, (s + k) % 4) for s in range(4)])  8.28 us
    pallas_call x1, Pallas kernels, near_branch(): call(functools.partial(early_kernel, first), [total_shape], [smem] + vm(2...  6.35 us
    pallas_call x1, Pallas kernels, near_branch(): call(functools.partial(couple_kernel, second), [total_shape, coupling_sha...  5.31 us
    pallas_call x1, Pallas kernels, shards(): call(solve_kernel, [shape((LEAF_PTS, SKEL), BF16)], vm(5) + [anywhere], v...  4.15 us
    pallas_call x1, Pallas kernels, near_branch(): call(own_kernel, [total_shape, shape((LEAF_DEV * LEAF_PTS, AUG), BF16)],...  4.11 us
  transfers between devices with their start and end apart: 13, of which 8 were waited for; matrix products, arithmetic and copies ran while one was open for 0% of the time, Pallas kernels for 23%

profile of v1, /device:TPU:123, one launch (start us, length us, event | category | flops | bytes accessed | tf_op | source)
XLA Modules:
  0.0 82.1 jit_solution(18024206206858071873)
XLA Ops:
  0.6 2.4 %shard_map.68 = (s32[128]{0:T(128)S(1)}, bf16[2,544,128]{2,1,0:T(8,128)(2,1)S(1)}, bf16[2,544,128]{2,1,0:T(8,128)(2,1)}, bf16[2,544,128]{2,1,0:T(8,128)(2,1)}, bf16[2,544,128]{2,1,0:T(8,128)(2,1)}) custom-call(s32[8,256]{1,0:T(8,128)} %bitcast.118, s32[256]{0:T(256)} %order_s.1, s32[8,256]{1,0:T(8,128)} %bitcast.119, s32[2,128]{1,0:T(2,128)} %bitcast.104, ...), custom_call_target="tpu_custom_call" | custom-call | tf_op jit(solution)/shard_map/pallas_call | solution.py:378
  3.1 51.2 %conditional.1 = (bf16[4,512,128]{2,1,0:T(8,128)(2,1)S(1)}, bf16[512,128]{1,0:T(8,128)(2,1)S(1)}, bf16[512,128]{1,0:T(8,128)(2,1)S(1)}, bf16[512,128]{1,0:T(8,12...) conditional(s32[]{:T(128)} %bitcast.33, (s32[256,8]{0,1:T(8,128)}, s32[256]{0:T(256)}, ...), branch_computations={%region_0.11_spmd, %region_11.12_spmd} | conditional | flops 597918080 | bytes 139693680 | solution.py:439
  3.4 2.6 %collective-permute-start = (bf16[2,544,128]{2,1,0:T(8,128)(2,1)S(1)}, bf16[2,544,128]{2,1,0:T(8,128)(2,1)S(1)}, u32[]{:S(2)}, u32[]{:S(2)}) collective-permute-start(bf16[2,544,128]{2,1,0:T(8,128)(2,1)S(1)} %get-tuple-element.76), channel_id=1, source_target_pairs={{248,0},{252,4},{0,8},{4,12},{8,16},{12,20},{16,24},{20,28},{24,32... | collective-permute-start | bytes 835592 | tf_op jit(solution)/shard_map/cond/branch_1_fun/ppermute | solution.py:397
  6.0 4.1 %branch_1_fun.5 = (f32[4,512,128]{2,1,0:T(8,128)S(1)}, bf16[2048,16]{1,0:T(8,128)(2,1)S(1)}) custom-call(s32[128]{0:T(128)S(1)} %get-tuple-element.70.table, bf16[8,2048]{1,0:T(8,128)(2,1)} %get-tuple-element.71.points, bf16[4,512,128]{2,1,0:T(8,128)(2,1)} %get-tuple-element.72.omega), custom_call_target="tpu_custom_call" | custom-call | tf_op jit(solution)/shard_map/cond/branch_1_fun/pallas_call | solution.py:402
  11.3 1.3 %branch_1_fun.6 = (bf16[8,512]{1,0:T(8,128)(2,1)S(1)}, bf16[2,560,128]{2,1,0:T(8,128)(2,1)S(1)}, bf16[2,544,128]{2,1,0:T(8,128)(2,1)S(1)}) custom-call(s32[128]{0:T(128)S(1)} %get-tuple-element.70.table, bf16[8,2048]{1,0:T(8,128)(2,1)} %get-tuple-element.71.points, bf16[4,512,128]{2,1,0:T(8,128)(2,1)} %get-tuple-element.72.omega, ...), custom_call_target="tpu_custom_call" | custom-call | tf_op jit(solution)/shard_map/cond/branch_1_fun/pallas_call | solution.py:405
  12.6 1.6 %collective-permute-start.1 = (bf16[2,560,128]{2,1,0:T(8,128)(2,1)S(1)}, bf16[2,560,128]{2,1,0:T(8,128)(2,1)S(1)}, u32[]{:S(2)}, u32[]{:S(2)}) collective-permute-start(bf16[2,560,128]{2,1,0:T(8,128)(2,1)S(1)} %get-tuple-element.77), channel_id=1, source_target_pairs={{4,0},{0,4},{12,8},{8,12},{20,16},{16,20},{28,24},{24,28},{36,32},... | collective-permute-start | bytes 860168 | tf_op jit(solution)/shard_map/cond/branch_1_fun/ppermute | solution.py:397
  14.2 5.5 %collective-permute-start.2 = (bf16[2,544,128]{2,1,0:T(8,128)(2,1)}, bf16[2,544,128]{2,1,0:T(8,128)(2,1)S(1)}, u32[]{:S(2)}, u32[]{:S(2)}) collective-permute-start(bf16[2,544,128]{2,1,0:T(8,128)(2,1)} %get-tuple-element.78), channel_id=1, source_target_pairs={{252,0},{248,4},{4,8},{0,12},{12,16},{8,20},{20,24},{16,28},{28,32... | collective-permute-start | bytes 835592 | tf_op jit(solution)/shard_map/cond/branch_1_fun/ppermute | solution.py:397
  19.7 1.6 %collective-permute-start.4 = (bf16[2,544,128]{2,1,0:T(8,128)(2,1)}, bf16[2,544,128]{2,1,0:T(8,128)(2,1)S(1)}, u32[]{:S(2)}, u32[]{:S(2)}) collective-permute-start(bf16[2,544,128]{2,1,0:T(8,128)(2,1)} %get-tuple-element.81), channel_id=1, source_target_pairs={{244,0},{8,4},{252,8},{16,12},{4,16},{24,20},{12,24},{32,28},{20,3... | collective-permute-start | bytes 835592 | tf_op jit(solution)/shard_map/cond/branch_1_fun/ppermute | solution.py:397
  21.2 1.7 %collective-permute-start.5 = (bf16[2,544,128]{2,1,0:T(8,128)(2,1)S(1)}, bf16[2,544,128]{2,1,0:T(8,128)(2,1)S(1)}, u32[]{:S(2)}, u32[]{:S(2)}) collective-permute-start(bf16[2,544,128]{2,1,0:T(8,128)(2,1)S(1)} %get-tuple-element.83), channel_id=1, source_target_pairs={{128,0},{132,4},{136,8},{140,12},{144,16},{148,20},{152,24},{156,2... | collective-permute-start | bytes 835592 | tf_op jit(solution)/shard_map/cond/branch_1_fun/ppermute | solution.py:397
  22.9 8.4 %collective-permute-done.2.rest_2_ = bf16[2,544,128]{2,1,0:T(8,128)(2,1)S(1)} collective-permute-done((bf16[2,544,128]{2,1,0:T(8,128)(2,1)}, bf16[2,544,128]{2,1,0:T(8,128)(2,1)S(1)}, u32[]{:S(2)}, u32[]{:S(2)}) %collective-permute-start.2) | collective-permute-done | bytes 278560 | tf_op jit(solution)/shard_map/cond/branch_1_fun/ppermute | solution.py:397
  31.4 6.3 %branch_1_fun.7.before = f32[4,512,128]{2,1,0:T(8,128)S(1)} custom-call(s32[128]{0:T(128)S(1)} %get-tuple-element.70.table, bf16[2048,16]{1,0:T(8,128)(2,1)S(1)} %get-tuple-element.73.left, f32[4,512,128]{2,1,0:T(8,128)S(1)} %get-tuple-element.74.before, bf16[2,560,128]{2,1,0:T(8,128)(2,1)S(1)} %collective-permute-done.1.rest_0_.beside, ...), custom_call_target="tpu_custom_call" | custom-call | tf_op jit(solution)/shard_map/cond/branch_1_fun/pallas_call | solution.py:414
  37.7 9.1 %collective-permute-done.4.rest_1_ = bf16[2,544,128]{2,1,0:T(8,128)(2,1)S(1)} collective-permute-done((bf16[2,544,128]{2,1,0:T(8,128)(2,1)}, bf16[2,544,128]{2,1,0:T(8,128)(2,1)S(1)}, u32[]{:S(2)}, u32[]{:S(2)}) %collective-permute-start.4) | collective-permute-done | bytes 278560 | tf_op jit(solution)/shard_map/cond/branch_1_fun/ppermute | solution.py:397
  46.8 5.3 %branch_1_fun.8 = (f32[4,512,128]{2,1,0:T(8,128)S(1)}, bf16[512,512]{1,0:T(8,128)(2,1)S(1)}) custom-call(s32[128]{0:T(128)S(1)} %get-tuple-element.70.table, bf16[2048,16]{1,0:T(8,128)(2,1)S(1)} %get-tuple-element.73.left, f32[4,512,128]{2,1,0:T(8,128)S(1)} %branch_1_fun.7.before, bf16[8,512]{1,0:T(8,128)(2,1)S(1)} %get-tuple-element.79.skeleton, ...), custom_call_target="tpu_custom_call" | custom-call | tf_op jit(solution)/shard_map/cond/branch_1_fun/pallas_call | solution.py:417
  52.2 2.1 %branch_1_fun.9 = (bf16[4,512,128]{2,1,0:T(8,128)(2,1)S(1)}, bf16[512,128]{1,0:T(8,128)(2,1)S(1)}, bf16[512,128]{1,0:T(8,128)(2,1)S(1)}, bf16[512,128]{1,0:T(8,128)(2,1)S(1)}, bf16[512,128]{1,0:T(8,128)(2,1)S(1)}) custom-call(s32[128]{0:T(128)S(1)} %get-tuple-element.70.table, bf16[2048,16]{1,0:T(8,128)(2,1)S(1)} %get-tuple-element.73.left, ...), custom_call_target="tpu_custom_call" | custom-call | tf_op jit(solution)/shard_map/cond/branch_1_fun/pallas_call | solution.py:420
  54.3 1.3 %collective-permute-start.7 = (bf16[512,128]{1,0:T(8,128)(2,1)S(1)}, bf16[512,128]{1,0:T(8,128)(2,1)S(1)}, u32[]{:S(2)}, u32[]{:S(2)}) collective-permute-start(bf16[512,128]{1,0:T(8,128)(2,1)S(1)} %get-tuple-element.109.b1), channel_id=1, source_target_pairs={{0,1},{1,2},{2,3},{3,0},{4,5},{5,6},{6,7},{7,4},{8,9},{9,10},{10,1... | collective-permute-start | bytes 393224 | tf_op jit(solution)/shard_map/ppermute | solution.py:387
  56.4 1.9 %collective-permute-start.9 = (bf16[512,128]{1,0:T(8,128)(2,1)S(1)}, bf16[512,128]{1,0:T(8,128)(2,1)S(1)}, u32[]{:S(2)}, u32[]{:S(2)}) collective-permute-start(bf16[512,128]{1,0:T(8,128)(2,1)S(1)} %get-tuple-element.111.b3), channel_id=1, source_target_pairs={{0,3},{1,0},{2,1},{3,2},{4,7},{5,4},{6,5},{7,6},{8,11},{9,8},{10,9... | collective-permute-start | bytes 393224 | tf_op jit(solution)/shard_map/ppermute | solution.py:387
  59.5 2.4 %collective-permute-done.8.b2 = bf16[512,128]{1,0:T(8,128)(2,1)S(1)} collective-permute-done((bf16[512,128]{1,0:T(8,128)(2,1)S(1)}, bf16[512,128]{1,0:T(8,128)(2,1)S(1)}, u32[]{:S(2)}, u32[]{:S(2)}) %collective-permute-start.8) | collective-permute-done | bytes 131104 | tf_op jit(solution)/shard_map/ppermute | solution.py:387
  61.9 2.1 %collective-permute-done.9.b3 = bf16[512,128]{1,0:T(8,128)(2,1)S(1)} collective-permute-done((bf16[512,128]{1,0:T(8,128)(2,1)S(1)}, bf16[512,128]{1,0:T(8,128)(2,1)S(1)}, u32[]{:S(2)}, u32[]{:S(2)}) %collective-permute-start.9) | collective-permute-done | bytes 131104 | tf_op jit(solution)/shard_map/ppermute | solution.py:387
  64.0 4.2 %shard_map.70.i0.rest_0_ = bf16[512,128]{1,0:T(8,128)(2,1)S(1)} custom-call(bf16[512,128]{1,0:T(8,128)(2,1)S(1)} %get-tuple-element.108.b0, bf16[512,128]{1,0:T(8,128)(2,1)S(1)} %collective-permute-done.7.b1, bf16[512,128]{1,0:T(8,128)(2,1)S(1)} %collective-permute-done.8.b2, bf16[512,128]{1,0:T(8,128)(2,1)S(1)} %collective-permute-done.9.b3, ...), custom_call_target="tpu_custom_call" | custom-call | tf_op jit(solution)/shard_map/pallas_call | solution.py:444
  68.2 1.4 %collective-permute-start.10 = (bf16[512,128]{1,0:T(8,128)(2,1)S(1)}, bf16[512,128]{1,0:T(8,128)(2,1)S(1)}, u32[]{:S(2)}, u32[]{:S(2)}) collective-permute-start(bf16[512,128]{1,0:T(8,128)(2,1)S(1)} %shard_map.70.i0.rest_0_), channel_id=1, source_target_pairs={{0,1},{1,2},{2,3},{3,0},{4,5},{5,6},{6,7},{7,4},{8,9},{9,10},{10,1... | collective-permute-start | bytes 393224 | tf_op jit(solution)/shard_map/ppermute | solution.py:387
  69.5 1.5 %collective-permute-start.11 = (bf16[512,128]{1,0:T(8,128)(2,1)S(1)}, bf16[512,128]{1,0:T(8,128)(2,1)S(1)}, u32[]{:S(2)}, u32[]{:S(2)}) collective-permute-start(bf16[512,128]{1,0:T(8,128)(2,1)S(1)} %shard_map.70.i0.rest_0_), channel_id=1, source_target_pairs={{0,2},{1,3},{2,0},{3,1},{4,6},{5,7},{6,4},{7,5},{8,10},{9,11},{10,... | collective-permute-start | bytes 393224 | tf_op jit(solution)/shard_map/ppermute | solution.py:387
  71.0 1.4 %collective-permute-start.12 = (bf16[512,128]{1,0:T(8,128)(2,1)S(1)}, bf16[512,128]{1,0:T(8,128)(2,1)S(1)}, u32[]{:S(2)}, u32[]{:S(2)}) collective-permute-start(bf16[512,128]{1,0:T(8,128)(2,1)S(1)} %shard_map.70.i0.rest_0_), channel_id=1, source_target_pairs={{0,3},{1,0},{2,1},{3,2},{4,7},{5,4},{6,5},{7,6},{8,11},{9,8},{10,9... | collective-permute-start | bytes 393224 | tf_op jit(solution)/shard_map/ppermute | solution.py:387
  72.4 1.3 %shard_map.72.rest_0_ = bf16[512,128]{1,0:T(8,128)(2,1)S(1)} custom-call(bf16[4,512,128]{2,1,0:T(8,128)(2,1)} %bitcast.107, bf16[512,128]{1,0:T(8,128)(2,1)S(1)} %shard_map.70.i0.rest_0_), custom_call_target="tpu_custom_call" | custom-call | tf_op jit(solution)/shard_map/pallas_call | solution.py:449
  75.0 3.9 %collective-permute-done.12.i3.rest_3_ = bf16[512,128]{1,0:T(8,128)(2,1)S(1)} collective-permute-done((bf16[512,128]{1,0:T(8,128)(2,1)S(1)}, bf16[512,128]{1,0:T(8,128)(2,1)S(1)}, u32[]{:S(2)}, u32[]{:S(2)}) %collective-permute-start.12) | collective-permute-done | bytes 131104 | tf_op jit(solution)/shard_map/ppermute | solution.py:387
  (19 shorter events, 7.7 us)
Async XLA Ops:
  3.1 60.9 %copy-start.4 = (s32[4,128]{1,0:T(4,128)S(1)}, s32[4,128]{1,0:T(4,128)}, u32[]{:S(2)}) copy-start(s32[4,128]{1,0:T(4,128)} %pivots.3) | copy-start | bytes 6148
  3.1 75.7 %copy-start.1 = (bf16[2048,128]{1,0:T(8,128)(2,1)S(1)}, bf16[2048,128]{1,0:T(8,128)(2,1)}, u32[]{:S(2)}) copy-start(bf16[2048,128]{1,0:T(8,128)(2,1)} %param.10) | copy-start | bytes 1572868
  3.4 7.9 %collective-permute-start = (bf16[2,544,128]{2,1,0:T(8,128)(2,1)S(1)}, bf16[2,544,128]{2,1,0:T(8,128)(2,1)S(1)}, u32[]{:S(2)}, u32[]{:S(2)}) collective-permute-start(bf16[2,544,128]{2,1,0:T(8,128)(2,1)S(1)} %get-tuple-element.76), channel_id=1, source_target_pairs={{248,0},{252,4},{0,8},{4,12},{8,16},{12,20},{16,24},{20,28},{24,32... | collective-permute-start | bytes 835592 | tf_op jit(solution)/shard_map/cond/branch_1_fun/ppermute | solution.py:397
  12.6 18.8 %collective-permute-start.1 = (bf16[2,560,128]{2,1,0:T(8,128)(2,1)S(1)}, bf16[2,560,128]{2,1,0:T(8,128)(2,1)S(1)}, u32[]{:S(2)}, u32[]{:S(2)}) collective-permute-start(bf16[2,560,128]{2,1,0:T(8,128)(2,1)S(1)} %get-tuple-element.77), channel_id=1, source_target_pairs={{4,0},{0,4},{12,8},{8,12},{20,16},{16,20},{28,24},{24,28},{36,32},... | collective-permute-start | bytes 860168 | tf_op jit(solution)/shard_map/cond/branch_1_fun/ppermute | solution.py:397
  14.2 17.2 %collective-permute-start.2 = (bf16[2,544,128]{2,1,0:T(8,128)(2,1)}, bf16[2,544,128]{2,1,0:T(8,128)(2,1)S(1)}, u32[]{:S(2)}, u32[]{:S(2)}) collective-permute-start(bf16[2,544,128]{2,1,0:T(8,128)(2,1)} %get-tuple-element.78), channel_id=1, source_target_pairs={{252,0},{248,4},{4,8},{0,12},{12,16},{8,20},{20,24},{16,28},{28,32... | collective-permute-start | bytes 835592 | tf_op jit(solution)/shard_map/cond/branch_1_fun/ppermute | solution.py:397
  19.7 18.1 %collective-permute-start.3 = (bf16[2,544,128]{2,1,0:T(8,128)(2,1)}, bf16[2,544,128]{2,1,0:T(8,128)(2,1)S(1)}, u32[]{:S(2)}, u32[]{:S(2)}) collective-permute-start(bf16[2,544,128]{2,1,0:T(8,128)(2,1)} %get-tuple-element.80), channel_id=1, source_target_pairs={{8,0},{12,4},{16,8},{20,12},{24,16},{28,20},{32,24},{36,28},{40,32... | collective-permute-start | bytes 835592 | tf_op jit(solution)/shard_map/cond/branch_1_fun/ppermute | solution.py:397
  19.7 27.2 %collective-permute-start.4 = (bf16[2,544,128]{2,1,0:T(8,128)(2,1)}, bf16[2,544,128]{2,1,0:T(8,128)(2,1)S(1)}, u32[]{:S(2)}, u32[]{:S(2)}) collective-permute-start(bf16[2,544,128]{2,1,0:T(8,128)(2,1)} %get-tuple-element.81), channel_id=1, source_target_pairs={{244,0},{8,4},{252,8},{16,12},{4,16},{24,20},{12,24},{32,28},{20,3... | collective-permute-start | bytes 835592 | tf_op jit(solution)/shard_map/cond/branch_1_fun/ppermute | solution.py:397
  21.2 30.9 %collective-permute-start.5 = (bf16[2,544,128]{2,1,0:T(8,128)(2,1)S(1)}, bf16[2,544,128]{2,1,0:T(8,128)(2,1)S(1)}, u32[]{:S(2)}, u32[]{:S(2)}) collective-permute-start(bf16[2,544,128]{2,1,0:T(8,128)(2,1)S(1)} %get-tuple-element.83), channel_id=1, source_target_pairs={{128,0},{132,4},{136,8},{140,12},{144,16},{148,20},{152,24},{156,2... | collective-permute-start | bytes 835592 | tf_op jit(solution)/shard_map/cond/branch_1_fun/ppermute | solution.py:397
  54.3 5.2 %collective-permute-start.7 = (bf16[512,128]{1,0:T(8,128)(2,1)S(1)}, bf16[512,128]{1,0:T(8,128)(2,1)S(1)}, u32[]{:S(2)}, u32[]{:S(2)}) collective-permute-start(bf16[512,128]{1,0:T(8,128)(2,1)S(1)} %get-tuple-element.109.b1), channel_id=1, source_target_pairs={{0,1},{1,2},{2,3},{3,0},{4,5},{5,6},{6,7},{7,4},{8,9},{9,10},{10,1... | collective-permute-start | bytes 393224 | tf_op jit(solution)/shard_map/ppermute | solution.py:387
  55.6 6.3 %collective-permute-start.8 = (bf16[512,128]{1,0:T(8,128)(2,1)S(1)}, bf16[512,128]{1,0:T(8,128)(2,1)S(1)}, u32[]{:S(2)}, u32[]{:S(2)}) collective-permute-start(bf16[512,128]{1,0:T(8,128)(2,1)S(1)} %get-tuple-element.110.b2), channel_id=1, source_target_pairs={{0,2},{1,3},{2,0},{3,1},{4,6},{5,7},{6,4},{7,5},{8,10},{9,11},{10,... | collective-permute-start | bytes 393224 | tf_op jit(solution)/shard_map/ppermute | solution.py:387
  56.4 7.6 %collective-permute-start.9 = (bf16[512,128]{1,0:T(8,128)(2,1)S(1)}, bf16[512,128]{1,0:T(8,128)(2,1)S(1)}, u32[]{:S(2)}, u32[]{:S(2)}) collective-permute-start(bf16[512,128]{1,0:T(8,128)(2,1)S(1)} %get-tuple-element.111.b3), channel_id=1, source_target_pairs={{0,3},{1,0},{2,1},{3,2},{4,7},{5,4},{6,5},{7,6},{8,11},{9,8},{10,9... | collective-permute-start | bytes 393224 | tf_op jit(solution)/shard_map/ppermute | solution.py:387
  68.2 5.6 %collective-permute-start.10 = (bf16[512,128]{1,0:T(8,128)(2,1)S(1)}, bf16[512,128]{1,0:T(8,128)(2,1)S(1)}, u32[]{:S(2)}, u32[]{:S(2)}) collective-permute-start(bf16[512,128]{1,0:T(8,128)(2,1)S(1)} %shard_map.70.i0.rest_0_), channel_id=1, source_target_pairs={{0,1},{1,2},{2,3},{3,0},{4,5},{5,6},{6,7},{7,4},{8,9},{9,10},{10,1... | collective-permute-start | bytes 393224 | tf_op jit(solution)/shard_map/ppermute | solution.py:387
  69.5 5.4 %collective-permute-start.11 = (bf16[512,128]{1,0:T(8,128)(2,1)S(1)}, bf16[512,128]{1,0:T(8,128)(2,1)S(1)}, u32[]{:S(2)}, u32[]{:S(2)}) collective-permute-start(bf16[512,128]{1,0:T(8,128)(2,1)S(1)} %shard_map.70.i0.rest_0_), channel_id=1, source_target_pairs={{0,2},{1,3},{2,0},{3,1},{4,6},{5,7},{6,4},{7,5},{8,10},{9,11},{10,... | collective-permute-start | bytes 393224 | tf_op jit(solution)/shard_map/ppermute | solution.py:387
  71.0 7.8 %collective-permute-start.12 = (bf16[512,128]{1,0:T(8,128)(2,1)S(1)}, bf16[512,128]{1,0:T(8,128)(2,1)S(1)}, u32[]{:S(2)}, u32[]{:S(2)}) collective-permute-start(bf16[512,128]{1,0:T(8,128)(2,1)S(1)} %shard_map.70.i0.rest_0_), channel_id=1, source_target_pairs={{0,3},{1,0},{2,1},{3,2},{4,7},{5,4},{6,5},{7,6},{8,11},{9,8},{10,9... | collective-permute-start | bytes 393224 | tf_op jit(solution)/shard_map/ppermute | solution.py:387
  79.2 1.9 %collective-permute-start.13 = (bf16[512,128]{1,0:T(8,128)(2,1)S(1)}, bf16[512,128]{1,0:T(8,128)(2,1)S(1)}, u32[]{:S(2)}, u32[]{:S(2)}) collective-permute-start(bf16[512,128]{1,0:T(8,128)(2,1)S(1)} %shard_map.73), channel_id=1, source_target_pairs={{0,4},{4,0},{8,12},{12,8},{16,20},{20,16},{24,28},{28,24},{32,36},... | collective-permute-start | bytes 393224 | tf_op jit(solution)/shard_map/ppermute | solution.py:455
